TPU v7x, 32 devices: a whole 2x2x4 slice. The times are simulated.
32 devices in a mesh: ctx: 16 (over z, y, x), head: 2 (over core).
Axes of the slice: x: 2, y: 2, z: 4, core: 2. Of those that a mesh axis runs over, the one named last changes fastest.
Arguments:
- queries: bfloat16 [2048, 32, 128], P('ctx', 'head'), may hold values from -190 to 190
- keys: bfloat16 [2048, 8, 128], P('ctx', 'head'), may hold values from -6.2 to 6.2
- values: bfloat16 [2048, 8, 128], P('ctx', 'head'), may hold values from -16 to 16
- feature_weight: float32 [32, 128, 128], P('head'), may hold values from -0.5 to 0.5
Outputs:
- student: bfloat16 [2048, 32, 128], P('ctx', 'head')
- update: float32 [32, 128, 128], P('head')
All inputs are finite; a program needn't handle non-finite values.
Results may differ from a plain program's by a relative error of at most 0.003.
The roundings to bfloat16 on the way count: a program that leaves them out, or rounds other values in their place, can miss the bound.
Values may be sent and summed in bfloat16 or wider, within the bound.
A program may use at most 64 MiB of HBM per device.

v0:
```python
import math

import jax
import jax.numpy as jnp
from jax import lax
from jax.sharding import PartitionSpec as P

precise = lax.Precision.HIGHEST
big_negative = -1e30


def shifted(shard, axis, by):
    devices = lax.axis_size(axis)
    pairs = [(i, i + by) for i in range(devices) if 0 <= i + by < devices]
    return lax.ppermute(shard, axis, pairs)


def carried_in(part, axis, combine, identity):
    count = lax.axis_size(axis)
    place = lax.axis_index(axis)
    ahead = count - 1 - place
    gathered = jax.tree.map(lambda a: lax.all_gather(a, axis), part)
    state = jax.tree.map(lambda a, e: jnp.zeros_like(a) + jnp.asarray(e, a.dtype), part, identity)

    def one(step, state):
        source = count - 1 - step
        return combine(
            state, jax.tree.map(lambda a: lax.dynamic_index_in_dim(a, source, 0, False), gathered)
        )

    return lax.fori_loop(0, ahead, one, state)


def feature_map(projection):
    return jnp.concatenate(
        [jax.nn.softmax(projection, axis=-1), jax.nn.softmax(-projection, axis=-1)], axis=-1
    )


def feature_pull(projection, upstream):
    half_len = upstream.shape[-1] // 2
    upper = jax.nn.softmax(projection, axis=-1)
    lower = jax.nn.softmax(-projection, axis=-1)
    grad_upper = upstream[..., :half_len]
    grad_lower = upstream[..., half_len:]
    upper_part = upper * (grad_upper - jnp.sum(upper * grad_upper, axis=-1, keepdims=True))
    lower_part = lower * (grad_lower - jnp.sum(lower * grad_lower, axis=-1, keepdims=True))
    return upper_part - lower_part


def add_pair(earlier, later):
    return (earlier[0] + later[0], earlier[1] + later[1])


def skip_block(carry_in):
    return carry_in


def shards(queries, keys, values, feature_weight):
    block_len, head_count, head_width = queries.shape
    kv_count = keys.shape[1]
    group_size = head_count // kv_count
    feature_len = feature_weight.shape[2] // 2
    my_block = lax.axis_index("ctx")
    score_scale = 1.0 / math.sqrt(head_width)
    grouped_q = queries.reshape(block_len, kv_count, group_size, head_width)
    maps_weight = feature_weight.reshape(kv_count, group_size, head_width, 2 * feature_len)
    query_map = maps_weight[..., :feature_len]
    key_map = maps_weight[..., feature_len:]
    query_pos = my_block * block_len + jnp.arange(block_len, dtype=jnp.int32)
    prev_start = (my_block - 1) * block_len
    last_row = my_block * block_len + block_len - 1
    initial = [
        jnp.full((kv_count, group_size, block_len), big_negative, jnp.float32),
        jnp.zeros((kv_count, group_size, block_len), jnp.float32),
        jnp.zeros((kv_count, group_size, block_len, head_width), jnp.float32),
    ]
    initial = initial + [
        jnp.zeros((kv_count, group_size, 2 * feature_len, head_width), jnp.float32),
        jnp.zeros((kv_count, group_size, 2 * feature_len), jnp.float32),
    ]
    initial = tuple(initial)
    piece_keys = lax.all_gather(keys, "ctx", axis=0, tiled=True)
    piece_values = lax.all_gather(values, "ctx", axis=0, tiled=True)
    piece_rows = piece_keys.shape[0]
    step_rows = math.gcd(piece_rows, 512)

    def attend(step_index, running):
        first_row = step_index * step_rows
        block_keys = lax.dynamic_slice_in_dim(piece_keys, step_index * step_rows, step_rows, 0)
        block_values = lax.dynamic_slice_in_dim(piece_values, step_index * step_rows, step_rows, 0)
        key_pos = first_row + jnp.arange(step_rows, dtype=jnp.int32)

        def compute(carry_in):
            row_max, running_sum, accumulated = (carry_in[0], carry_in[1], carry_in[2])
            scores = (
                jnp.einsum(
                    "tkgd,skd->kgts", grouped_q, block_keys, preferred_element_type=jnp.float32
                )
                * score_scale
            )
            allowed = key_pos[None, :] <= query_pos[:, None]
            scores = jnp.where(allowed, scores, big_negative)
            new_max = jnp.maximum(row_max, jnp.max(scores, axis=-1))
            attn_weight = jnp.where(allowed, jnp.exp(scores - new_max[..., None]), 0.0)
            factor = jnp.exp(row_max - new_max)
            running_sum = running_sum * factor + jnp.sum(attn_weight, axis=-1)
            accumulated = accumulated * factor[..., None] + jnp.einsum(
                "kgts,skd->kgtd",
                attn_weight.astype(jnp.bfloat16),
                block_values,
                preferred_element_type=jnp.float32,
            )
            result = [new_max, running_sum, accumulated] + list(carry_in[3:])
            in_state = (key_pos < prev_start).astype(jnp.float32)
            features = feature_map(
                jnp.einsum(
                    "skd,kgdf->kgsf", block_keys.astype(jnp.float32), key_map, precision=precise
                )
            )
            features = features * in_state[None, None, :, None]
            result[-2] = carry_in[-2] + jnp.einsum(
                "kgsf,skd->kgfd", features, block_values.astype(jnp.float32), precision=precise
            )
            result[-1] = carry_in[-1] + jnp.sum(features, axis=2)
            return tuple(result)

        return lax.cond(first_row <= last_row, compute, skip_block, running)

    folded = lax.fori_loop(0, piece_rows // step_rows, attend, initial)
    teacher = folded[2] / folded[1][..., None]
    stacked = jnp.stack([keys, values])
    moved = shifted(stacked, "ctx", 1)
    prev_keys, prev_values = (moved[0], moved[1])
    has_prev = (my_block > 0).astype(jnp.float32)
    window_keys = jnp.concatenate([prev_keys, keys], axis=0)
    window_values = jnp.concatenate([prev_values, values], axis=0)
    column = jnp.arange(2 * block_len, dtype=jnp.int32)
    row_index = jnp.arange(block_len, dtype=jnp.int32)
    allowed = (column[None, :] < block_len) & (my_block > 0) | (column[None, :] >= block_len) & (
        column[None, :] - block_len <= row_index[:, None]
    )
    scores = (
        jnp.einsum("tkgd,skd->kgts", grouped_q, window_keys, preferred_element_type=jnp.float32)
        * score_scale
    )
    scores = jnp.where(allowed, scores, big_negative)
    row_max = jnp.max(scores, axis=-1)
    window_weight = jnp.where(allowed, jnp.exp(scores - row_max[..., None]), 0.0)
    window_den = jnp.sum(window_weight, axis=-1)
    window_num = jnp.einsum(
        "kgts,skd->kgtd",
        window_weight.astype(jnp.bfloat16),
        window_values,
        preferred_element_type=jnp.float32,
    )
    key_proj = jnp.einsum(
        "skd,kgdf->kgsf", prev_keys.astype(jnp.float32), key_map, precision=precise
    )
    state, norm = (folded[-2], folded[-1])
    query_proj = jnp.einsum(
        "tkgd,kgdf->kgtf", grouped_q.astype(jnp.float32), query_map, precision=precise
    )
    query_feats = feature_map(query_proj)
    decay = jnp.exp(-row_max)
    far_num = decay[..., None] * jnp.einsum(
        "kgtf,kgfd->kgtd", query_feats, state, precision=precise
    )
    far_den = decay * jnp.einsum("kgtf,kgf->kgt", query_feats, norm, precision=precise)
    denominator = window_den + far_den
    mix = (window_num + far_num) / denominator[..., None]
    student = jnp.transpose(mix.astype(jnp.bfloat16), (2, 0, 1, 3)).reshape(
        block_len, head_count, head_width
    )
    mismatch = mix - teacher
    grad_num = mismatch / denominator[..., None]
    grad_den = -jnp.sum(mismatch * mix, axis=-1) / denominator
    lifted = decay[..., None] * query_feats
    grad_state = jnp.einsum("kgtf,kgtd->kgfd", lifted, grad_num, precision=precise)
    grad_norm = jnp.einsum("kgtf,kgt->kgf", lifted, grad_den, precision=precise)
    grad_qfeat = decay[..., None] * (
        jnp.einsum("kgfd,kgtd->kgtf", state, grad_num, precision=precise)
        + norm[:, :, None, :] * grad_den[..., None]
    )
    later_state, later_norm = carried_in(
        (grad_state, grad_norm),
        "ctx",
        add_pair,
        (jnp.zeros_like(grad_state), jnp.zeros_like(grad_norm)),
    )
    grad_kfeat = (
        jnp.einsum(
            "kgfd,skd->kgsf", later_state, prev_values.astype(jnp.float32), precision=precise
        )
        + later_norm[:, :, None, :]
    ) * has_prev
    grad_query = jnp.einsum(
        "tkgd,kgtf->kgdf",
        grouped_q.astype(jnp.float32),
        feature_pull(query_proj, grad_qfeat),
        precision=precise,
    )
    grad_key = jnp.einsum(
        "skd,kgsf->kgdf",
        prev_keys.astype(jnp.float32),
        feature_pull(key_proj, grad_kfeat),
        precision=precise,
    )
    gradients = jnp.concatenate([grad_query, grad_key], axis=-1).reshape(
        head_count, head_width, 2 * feature_len
    )
    entry_count = gradients.size * lax.axis_size("head")
    summed = lax.psum(gradients, "ctx")
    squares = lax.psum(jnp.sum(summed * summed), "head")
    update = summed / jnp.sqrt(squares / entry_count + 1e-06)
    return (student, update)


def solution(mesh):
    return jax.shard_map(
        shards,
        mesh=mesh,
        in_specs=(
            P("ctx", "head", None),
            P("ctx", "head", None),
            P("ctx", "head", None),
            P("head", None, None),
        ),
        out_specs=(P("ctx", "head", None), P("head", None, None)),
        check_vma=False,
    )
```

profile of v0, /device:TPU:0, one launch (start us, length us, event | category | flops | bytes accessed | tf_op | source)
XLA Modules:
  0.0 569.1 jit_solution(6820998690177619679)
XLA Ops:
  7.2 1.8 copy_bitcast_fusion
  10.6 4.9 collective-permute-start
  15.5 1.2 copy.28
  17.3 1.1 fusion.68
  20.3 1.0 collective-permute-done
  22.4 1.6 fusion.54
  24.0 50.8 %all-gather.6.cloned.1.call-done = bf16[2048,4,128]{2,0,1:T(8,128)(2,1)} async-done(((bf16[128,4,128]{2,0,1:T(8,128)(2,1)}), bf16[2048,4,128]{2,0,1:T(8,128)(2,1)}) %all-gather.6.cloned.1.call-update) | async-done | bytes 2097168 | tf_op jit(solution)/shard_map/all_gather | solution.py:83
  74.8 62.5 %all-gather.8.cloned.1.call-done = bf16[2048,4,128]{2,0,1:T(8,128)(2,1)} async-done(((bf16[128,4,128]{2,0,1:T(8,128)(2,1)}), bf16[2048,4,128]{2,0,1:T(8,128)(2,1)}) %all-gather.8.cloned.1.call-update) | async-done | bytes 2097168 | tf_op jit(solution)/shard_map/all_gather | solution.py:84
  137.2 1.1 broadcast.78.clone
  138.5 19.8 %while.37 = (s32[]{:T(128)}, f32[4,4,128]{2,1,0:T(4,128)S(1)}, f32[4,4,128]{2,1,0:T(4,128)S(1)}, f32[4,4,128,128]{3,2,1,0:T(8,128)}, f32[4,4,128,128]{3,2,1,0:T(...) while((s32[]{:T(128)}, f32[4,4,128]{2,1,0:T(4,128)S(1)}, ...), condition=%wide.region_15.16_spmd.clone, body=%wide.region_5.15_spmd.clone.sunk | while | flops 2976192000 | bytes 66634240 | solution.py:130
  138.5 19.5 %conditional.3 = ((f32[4,4,128]{2,1,0:T(4,128)S(1)}, f32[4,4,128]{2,1,0:T(4,128)S(1)}, f32[4,4,128,128]{3,2,1,0:T(8,128)}, f32[4,4,128,128]{3,2,1,0:T(8,128)S(1)}, f32[4,4,128]{2,1,0:T(4,128)S(1)})) conditional(s32[]{:T(128)} %convert_element_type.49, (f32[4,4,128]{2,1,0:T(4,128)S(1)}, f32[4,4,128]{2,1,0:T(4,128)S(1)}, f32[4,4,128,128]{3,2,1,0:T(8,128)}, ...), branch_computations={%region_6.0_spmd, %region_7.14_spmd} | conditional | flops 2976192000 | bytes 66631364 | solution.py:128
  138.5 2.0 fusion.25
  140.6 3.3 fusion.117
  143.9 3.3 fusion.116
  148.3 1.2 copy-done.5
  149.5 2.5 fusion.15
  152.2 1.8 fusion.4
  154.1 1.0 fusion.8
  155.3 1.7 fusion.16
  159.3 2.6 copy.37
  161.9 4.0 fusion.58
  166.9 3.5 fusion.66
  173.2 1.7 fusion.64
  174.9 99.0 %all-gather.1 = f32[64,4,128]{2,1,0:T(4,128)S(1)} all-gather(f32[4,4,128]{2,1,0:T(4,128)S(1)} %bitcast.194), channel_id=3, replica_groups=mesh['ctx'=16,'head'=2] {'ctx'}, dimensions={0}, use_global_device_ids=true | all-gather | bytes 139264 | tf_op jit(solution)/shard_map/all_gather | solution.py:22
  273.8 1.5 fusion.45
  276.1 143.0 %all-gather.10.cloned.1.call-done = f32[64,4,128,128]{3,2,1,0:T(8,128)} async-done(((f32[4,4,128,128]{3,2,1,0:T(8,128)}), f32[64,4,128,128]{3,2,1,0:T(8,128)}) %all-gather.10.cloned.1.call-update) | async-done | bytes 16777232 | tf_op jit(solution)/shard_map/all_gather | solution.py:22
  419.2 23.3 %while.36 = (s32[]{:T(128)}, f32[4,4,128,128]{3,2,1,0:T(8,128)S(1)}, f32[4,4,128]{2,1,0:T(4,128)S(1)}, s32[]{:T(128)}, f32[16,4,4,128,128]{4,3,2,1,0:T(8,128)}, ...) while((s32[]{:T(128)}, f32[4,4,128,128]{3,2,1,0:T(8,128)S(1)}, ...), condition=%wide.region_23.24_spmd, body=%wide.region_22.23_spmd.sunk | while | flops 264198 | bytes 3170459 | solution.py:31
  419.3 1.5 bitcast_add_fusion.5
  420.8 1.5 bitcast_add_fusion.5
  422.3 1.5 bitcast_add_fusion.5
  423.9 1.5 bitcast_add_fusion.5
  425.4 1.5 bitcast_add_fusion.5
  427.0 1.5 bitcast_add_fusion.5
  428.5 1.5 bitcast_add_fusion.5
  430.0 1.5 bitcast_add_fusion.5
  431.6 1.5 bitcast_add_fusion.5
  433.1 1.5 bitcast_add_fusion.5
  434.6 1.5 bitcast_add_fusion.5
  436.2 1.5 bitcast_add_fusion.5
  437.7 1.5 bitcast_add_fusion.5
  439.3 1.5 bitcast_add_fusion.5
  440.8 1.5 bitcast_add_fusion.5
  444.6 1.3 copy.40
  446.0 108.4 %all-reduce.2.cloned.1.call-done = f32[16,128,128]{2,1,0:T(8,128)} async-done(((f32[16,128,128]{2,1,0:T(8,128)}), f32[16,128,128]{2,1,0:T(8,128)}) %all-reduce.2.cloned.1.call-update) | async-done | bytes 1048592 | tf_op jit(solution)/shard_map/psum | solution.py:213
  554.3 2.2 multiply_reduce_fusion
  556.5 1.2 copy.41
  557.7 3.1 psum.15
  561.5 1.1 broadcast_divide_fusion.2
  (106 shorter events, 15.5 us)
Async XLA Ops:
  7.2 9.5 %copy-start.13 = (f32[16,128,128]{2,1,0:T(8,128)S(1)}, f32[16,128,128]{2,1,0:T(8,128)}, u32[]{:S(2)}) copy-start(f32[16,128,128]{2,1,0:T(8,128)} %param.13) | copy-start | bytes 3145732
  7.2 67.6 %all-gather.6.cloned.1.call-start = ((), (), s32[]{:S(2)}) async-start(), calls=%async_computation | async-start | bytes 2228224 | tf_op jit(solution)/shard_map/all_gather | solution.py:83
  9.1 128.2 %all-gather.8.cloned.1.call-start = ((), (), s32[]{:S(2)}) async-start(), calls=%async_computation.1 | async-start | bytes 2228224 | tf_op jit(solution)/shard_map/all_gather | solution.py:84
  9.8 409.3 %all-gather.10.cloned.1.call-start = ((), (), s32[]{:S(2)}) async-start(), calls=%async_computation.3 | async-start | bytes 17825792 | tf_op jit(solution)/shard_map/all_gather | solution.py:22
  10.6 10.7 %collective-permute-start = (bf16[2,128,4,128]{3,1,2,0:T(8,128)(2,1)}, bf16[2,128,4,128]{3,1,2,0:T(8,128)(2,1)S(1)}, u32[]{:S(2)}, u32[]{:S(2)}) collective-permute-start(bf16[2,128,4,128]{3,1,2,0:T(8,128)(2,1)} %pad_maximum_fusion.6), channel_id=1, source_target_pairs={{0,2},{2,4},{4,6},{6,8},{8,10},{10,12},{12,14},{14,16},{16,18},{18... | collective-permute-start | bytes 786440 | tf_op jit(solution)/shard_map/ppermute | solution.py:15
  19.3 2.1 copy-start.8
  21.4 1.0 copy-start.15
  147.9 1.6 copy-start.5
  154.1 1.2 copy-start.3
  157.0 1.0 copy-start.4
  161.9 5.0 copy-start
  161.9 5.0 copy-start.9
  165.9 1.0 copy-start.11
  170.4 383.9 %all-reduce.2.cloned.1.call-start = ((), (), s32[]{:S(2)}) async-start(), calls=%async_computation.2 | async-start | bytes 2097152 | tf_op jit(solution)/shard_map/psum | solution.py:213
  170.4 2.3 copy-start.1
  170.4 2.3 copy-start.10
  170.5 2.2 copy-start.12
  442.5 1.0 copy-start.6
  442.5 1.2 copy-start.7
  444.6 111.9 %copy-start.14 = (bf16[128,4,4,128]{0,3,2,1:T(8,128)(2,1)S(1)}, bf16[128,4,4,128]{0,3,2,1:T(8,128)(2,1)}, u32[]{:S(2)}) copy-start(bf16[128,4,4,128]{0,3,2,1:T(8,128)(2,1)} %get-tuple-element.586) | copy-start | bytes 1572868
  554.3 7.2 %copy-start.2 = (f32[16,128,128]{2,1,0:T(8,128)S(1)}, f32[16,128,128]{2,1,0:T(8,128)}, u32[]{:S(2)}) copy-start(f32[16,128,128]{2,1,0:T(8,128)} %all-reduce.2.cloned.1.call-done) | copy-start | bytes 3145732
Sparse Core Ops, SparseCore 0:
  10.8 63.9 all-gather.5
  77.5 59.6 all-gather.7
  170.5 248.5 all-gather.9
  446.1 108.2 all-reduce.1
where the time goes:
time: 570 us; the launch traced here: 569 us
  waiting for transfers between devices  366 us (64%)
  blocking collectives  102 us (18%)
  other arithmetic  40.9 us (7%)
  matrix products  25.1 us (4%)
  between operations  14.8 us (3%)
  local copies, waits for them, and re-layouts  13.7 us (2%)
    all_gather x1, waiting for transfers between devices, carried_in(): gathered = jax.tree.map(lambda a: lax.all_gather(a, axis), part)  143 us
    psum x1, waiting for transfers between devices, shards(): summed = lax.psum(gradients, 'ctx')  108 us
    all_gather x1, blocking collectives, carried_in(): gathered = jax.tree.map(lambda a: lax.all_gather(a, axis), part)  99 us
    all_gather x1, waiting for transfers between devices, shards(): piece_values = lax.all_gather(values, 'ctx', axis=0, tiled=True)  62.5 us
    all_gather x1, waiting for transfers between devices, shards(): piece_keys = lax.all_gather(keys, 'ctx', axis=0, tiled=True)  50.8 us
    add x30, other arithmetic, add_pair(): return (earlier[0] + later[0], earlier[1] + later[1])  22.6 us
  transfers between devices with their start and end apart: 5, of which 5 were waited for; matrix products, arithmetic and copies ran while one was open for 3% of the time, Pallas kernels for 0%

commit v1 on v0

--- a/solution.py
+++ b/solution.py
@@ -1,8 +1,11 @@
+import functools
 import math
 
 import jax
 import jax.numpy as jnp
 from jax import lax
+from jax.experimental import pallas as pl
+from jax.experimental.pallas import tpu as pltpu
 from jax.sharding import PartitionSpec as P
 
 precise = lax.Precision.HIGHEST
@@ -56,7 +59,7 @@
     return carry_in
 
 
-def shards(queries, keys, values, feature_weight):
+def general_shards(queries, keys, values, feature_weight):
     block_len, head_count, head_width = queries.shape
     kv_count = keys.shape[1]
     group_size = head_count // kv_count
@@ -216,6 +219,277 @@
     return (student, update)
 
 
+f32, bf16 = jnp.float32, jnp.bfloat16
+NN = (((1,), (0,)), ((), ()))
+NT = (((1,), (1,)), ((), ()))
+TN = (((0,), (0,)), ((), ()))
+
+
+def mxu(a, b, dims):
+    return lax.dot_general(a, b, dims, preferred_element_type=f32)
+
+
+def split(x, pieces):
+    out = []
+    for _ in range(pieces):
+        piece = x.astype(bf16)
+        out.append(piece)
+        x = x - piece.astype(f32)
+    return out
+
+
+def cat(parts, axis):
+    return jnp.concatenate(parts, axis=axis)
+
+
+def exact_by_wide(a, b, dims):
+    return mxu(cat([a, a], dims[0][0][0]), cat(split(b, 2), dims[0][1][0]), dims)
+
+
+def wide_by_exact(a, b, dims):
+    return mxu(cat(split(a, 2), dims[0][0][0]), cat([b, b], dims[0][1][0]), dims)
+
+
+def wide_by_wide(a, b, dims):
+    a_hi, a_lo = split(a, 2)
+    b_hi, b_lo = split(b, 2)
+    return mxu(
+        cat([a_hi, a_hi, a_lo], dims[0][0][0]), cat([b_hi, b_lo, b_hi], dims[0][1][0]), dims
+    )
+
+
+def half_sum(x, halves):
+    return wide_by_exact(x, halves, NN)
+
+
+def half_softmax(u, is_upper, halves):
+    top = jnp.max(jnp.where(is_upper, u, big_negative), axis=-1, keepdims=True)
+    low = jnp.max(jnp.where(is_upper, big_negative, u), axis=-1, keepdims=True)
+    e = jnp.exp(u - jnp.where(is_upper, top, low))
+    return e / half_sum(e, halves)
+
+
+def head_kernel(
+    x_ref, w_ref, student_ref, grad_ref,
+    score_ref, kfeat_ref, gstate_ref, gnorm_ref, state_ref, norm_ref, last_ref, lastn_ref,
+    wq_ref, wk_ref, acc_ref, peak_ref, total_ref, gq_ref, gk_ref,
+):
+    blocks, _, length, width = x_ref.shape
+    features = w_ref.shape[1] // 2
+    rows = 2 * length
+    steps = blocks // 2
+    scale = 1.0 / math.sqrt(width)
+    lane = lax.broadcasted_iota(jnp.int32, (rows, 2 * features), 1)
+    is_upper = lane < features
+    row_half = lax.broadcasted_iota(jnp.int32, (2 * features, 2 * features), 0) < features
+    col_half = lax.broadcasted_iota(jnp.int32, (2 * features, 2 * features), 1) < features
+    halves = jnp.where(row_half == col_half, 1.0, 0.0).astype(bf16)
+    w = w_ref[...]
+    wq, wk = w[:, :features], w[:, features:]
+    wq_ref[...] = cat(split(cat([wq, -wq], 1), 3), 0)
+    wk_ref[...] = cat(split(cat([wk, -wk], 1), 3), 0)
+    for ref in (state_ref, norm_ref, last_ref, lastn_ref, gq_ref, gk_ref):
+        ref[...] = jnp.zeros_like(ref)
+
+    def load(part, i):
+        return x_ref[pl.ds(2 * i, 2), part].reshape(rows, width)
+
+    def forward(i, carry):
+        q, k, v = load(0, i), load(1, i), load(2, i)
+        acc_ref[...] = jnp.zeros_like(acc_ref)
+        total_ref[...] = jnp.zeros_like(total_ref)
+        peak_ref[...] = jnp.full(peak_ref.shape, big_negative, f32)
+
+        def score(j, carry):
+            s = mxu(q, load(1, j), NT) * scale
+            score_ref[j] = s
+            peak_ref[...] = jnp.maximum(
+                peak_ref[...], jnp.maximum(s[:, :length], s[:, length:])
+            )
+            return carry
+
+        lax.fori_loop(0, i, score, 0)
+        s = mxu(q, k, NT) * scale
+        causal = lax.broadcasted_iota(jnp.int32, (rows, rows), 1) <= lax.broadcasted_iota(
+            jnp.int32, (rows, rows), 0
+        )
+        s = jnp.where(causal, s, big_negative)
+        score_ref[i] = s
+        row_max = jnp.max(
+            jnp.maximum(peak_ref[...], jnp.maximum(s[:, :length], s[:, length:])),
+            axis=-1,
+            keepdims=True,
+        )
+
+        def weigh(j, carry):
+            p = jnp.exp(score_ref[j] - row_max)
+            total_ref[...] += p[:, :length] + p[:, length:]
+            acc_ref[...] += mxu(p.astype(bf16), load(2, j), NN)
+            return carry
+
+        lax.fori_loop(0, i + 1, weigh, 0)
+        teacher = acc_ref[...] / jnp.sum(total_ref[...], axis=-1, keepdims=True)
+
+        before = jnp.maximum(i - 1, 0)
+        prev_top = score_ref[before, :length, length:]
+        prev_top = jnp.where(i > 0, prev_top, big_negative)
+        prev = cat([prev_top, s[length:, :length]], 0)
+        own = cat([s[:length, :length], s[length:, length:]], 0)
+        win_max = jnp.max(jnp.maximum(prev, own), axis=-1, keepdims=True)
+        p_prev, p_own = jnp.exp(prev - win_max), jnp.exp(own - win_max)
+        win_den = jnp.sum(p_prev + p_own, axis=-1, keepdims=True)
+        b_prev, b_own = p_prev.astype(bf16), p_own.astype(bf16)
+        v_before = x_ref[jnp.maximum(2 * i - 1, 0), 2]
+        win_num = cat(
+            [
+                mxu(cat([b_prev[:length], b_own[:length]], 1), cat([v_before, v[:length]], 0), NN),
+                mxu(cat([b_prev[length:], b_own[length:]], 1), v, NN),
+            ],
+            0,
+        )
+
+        qf = half_softmax(mxu(cat([q, q, q], 1), wq_ref[...], NN), is_upper, halves)
+        kf = half_softmax(mxu(cat([k, k, k], 1), wk_ref[...], NN), is_upper, halves)
+        kfeat_ref[i] = kf
+        own_0 = wide_by_exact(kf[:length], v[:length], TN)
+        own_1 = wide_by_exact(kf[length:], v[length:], TN)
+        sum_0 = jnp.sum(kf[:length], axis=0, keepdims=True)
+        sum_1 = jnp.sum(kf[length:], axis=0, keepdims=True)
+        state_0, norm_0 = state_ref[...], norm_ref[...]
+        state_1, norm_1 = state_0 + last_ref[...], norm_0 + lastn_ref[...]
+        state_ref[...], norm_ref[...] = state_1 + own_0, norm_1 + sum_0
+        last_ref[...], lastn_ref[...] = own_1, sum_1
+
+        norm = cat(
+            [
+                jnp.broadcast_to(norm_0, (length, 2 * features)),
+                jnp.broadcast_to(norm_1, (length, 2 * features)),
+            ],
+            0,
+        )
+        decay = jnp.exp(-win_max)
+        far = cat(
+            [wide_by_wide(qf[:length], state_0, NN), wide_by_wide(qf[length:], state_1, NN)], 0
+        )
+        den = win_den + decay * jnp.sum(qf * norm, axis=-1, keepdims=True)
+        mix = (win_num + decay * far) / den
+        student_ref[pl.ds(2 * i, 2)] = mix.astype(bf16).reshape(2, length, width)
+        mismatch = mix - teacher
+        g_num = mismatch / den
+        g_den = -jnp.sum(mismatch * mix, axis=-1, keepdims=True) / den
+        lifted = decay * qf
+        gstate_ref[2 * i] = wide_by_wide(lifted[:length], g_num[:length], TN)
+        gstate_ref[2 * i + 1] = wide_by_wide(lifted[length:], g_num[length:], TN)
+        pulled_norm = lifted * g_den
+        gnorm_ref[2 * i] = jnp.sum(pulled_norm[:length], axis=0, keepdims=True)
+        gnorm_ref[2 * i + 1] = jnp.sum(pulled_norm[length:], axis=0, keepdims=True)
+        g_qf = decay * (
+            cat(
+                [
+                    wide_by_wide(g_num[:length], state_0, NT),
+                    wide_by_wide(g_num[length:], state_1, NT),
+                ],
+                0,
+            )
+            + norm * g_den
+        )
+        d_q = qf * (g_qf - half_sum(qf * g_qf, halves))
+        gq_ref[...] += exact_by_wide(q, d_q, TN)
+        return carry
+
+    lax.fori_loop(0, steps, forward, 0)
+
+    for ref in (state_ref, norm_ref):
+        ref[...] = jnp.zeros_like(ref)
+
+    def backward(step, carry):
+        i = steps - 1 - step
+        k, v, kf = load(1, i), load(2, i), kfeat_ref[i]
+        nxt = jnp.minimum(i + 1, steps - 1)
+        live = jnp.where(step > 0, 1.0, 0.0)
+        later_1, later_n1 = state_ref[...], norm_ref[...]
+        later_0 = later_1 + live * gstate_ref[2 * nxt]
+        later_n0 = later_n1 + live * gnorm_ref[2 * nxt]
+        g_kf = cat(
+            [
+                exact_by_wide(v[:length], later_0, NT) + later_n0,
+                exact_by_wide(v[length:], later_1, NT) + later_n1,
+            ],
+            0,
+        )
+        d_k = kf * (g_kf - half_sum(kf * g_kf, halves))
+        gk_ref[...] += exact_by_wide(k, d_k, TN)
+        state_ref[...] = later_0 + gstate_ref[2 * i + 1]
+        norm_ref[...] = later_n0 + gnorm_ref[2 * i + 1]
+        return carry
+
+    lax.fori_loop(0, steps, backward, 0)
+    gq, gk = gq_ref[...], gk_ref[...]
+    grad_ref[...] = cat(
+        [gq[:, :features] - gq[:, features:], gk[:, :features] - gk[:, features:]], 1
+    )
+
+
+def whole_head(x, w):
+    blocks, _, length, width = x.shape
+    double = w.shape[1]
+    rows, steps = 2 * length, blocks // 2
+    vmem = pltpu.VMEM
+    return pl.pallas_call(
+        head_kernel,
+        out_shape=(
+            jax.ShapeDtypeStruct((blocks, length, width), bf16),
+            jax.ShapeDtypeStruct((width, double), f32),
+        ),
+        in_specs=[pl.BlockSpec(memory_space=vmem)] * 2,
+        out_specs=(pl.BlockSpec(memory_space=vmem),) * 2,
+        scratch_shapes=[
+            vmem((steps, rows, rows), f32),
+            vmem((steps, rows, double), f32),
+            vmem((blocks, double, width), f32),
+            vmem((blocks, 1, double), f32),
+            vmem((double, width), f32),
+            vmem((1, double), f32),
+            vmem((double, width), f32),
+            vmem((1, double), f32),
+            vmem((3 * width, double), bf16),
+            vmem((3 * width, double), bf16),
+            vmem((rows, width), f32),
+            vmem((rows, length), f32),
+            vmem((rows, length), f32),
+            vmem((width, double), f32),
+            vmem((width, double), f32),
+        ],
+        compiler_params=pltpu.CompilerParams(vmem_limit_bytes=40 * 2**20),
+    )(x, w)
+
+
+def head_shards(queries, keys, values, feature_weight):
+    block_len, head_count, head_width = queries.shape
+    group = head_count // keys.shape[1]
+    q = jnp.transpose(queries, (1, 0, 2))
+    k = jnp.repeat(jnp.transpose(keys, (1, 0, 2)), group, axis=0)
+    v = jnp.repeat(jnp.transpose(values, (1, 0, 2)), group, axis=0)
+    x = lax.all_to_all(jnp.stack([q, k, v], axis=1), "ctx", 0, 0)
+    w = lax.dynamic_index_in_dim(feature_weight, lax.axis_index("ctx"), 0, False)
+    mix, grad = whole_head(x, w)
+    student = jnp.transpose(lax.all_to_all(mix, "ctx", 0, 0), (1, 0, 2))
+    squares = lax.psum(jnp.sum(grad * grad), ("ctx", "head"))
+    gradients = lax.all_gather(grad, "ctx", axis=0)
+    entry_count = gradients.size * lax.axis_size("head")
+    update = gradients / jnp.sqrt(squares / entry_count + 1e-06)
+    return (student, update)
+
+
+def shards(queries, keys, values, feature_weight):
+    count = lax.axis_size("ctx")
+    width = queries.shape[2]
+    fits = queries.shape[1] == count and count % 2 == 0 and count * queries.shape[0] <= 4096
+    fits = fits and queries.shape[0] == width and feature_weight.shape[2] == width
+    body = head_shards if fits else general_shards
+    return body(queries, keys, values, feature_weight)
+
+
 def solution(mesh):
     return jax.shard_map(
         shards,

time: 570 us -> 156 us (0.27)
  waiting for transfers between devices: 366 us -> 40.9 us
  blocking collectives: 102 us -> 41 us
  other arithmetic: 40.9 us -> 5.03 us
  Pallas kernels: 0 us -> 33.1 us
  matrix products: 25.1 us -> 0 us
  starting transfers between devices: 5.03 us -> 16.1 us
  local copies, waits for them, and re-layouts: 13.7 us -> 4.46 us
    all_gather x3 -> x1, waiting for transfers between devices: 256 us -> 6.83 us  [head_shards(): gradients = lax.all_gather(grad, 'ctx', axis=0)]
    psum x1 -> x0, waiting for transfers between devices: 108 us -> none  [shards(): summed = lax.psum(gradients, 'ctx')]
    all_gather x1 -> x0, blocking collectives: 99 us -> none  [carried_in(): gathered = jax.tree.map(lambda a: lax.all_gather(a, axis), part)]
    psum x1, blocking collectives: 3.08 us -> 41 us  [head_shards(): squares = lax.psum(jnp.sum(grad * grad), ('ctx', 'head'))]
    all_to_all x0 -> x2, waiting for transfers between devices: none -> 34 us  [the longest x1 34 us: head_shards(): x = lax.all_to_all(jnp.stack([q, k, v], axis=1), 'ctx', 0, 0)]
    pallas_call x0 -> x1, Pallas kernels: none -> 33.1 us  [whole_head(): pl.pallas_call(head_kernel, out_shape=(jax.ShapeDtypeStruct((blocks, leng...]
    dot_general x14 -> x0, matrix products: 22.6 us -> none  [the longest x1 4.03 us: shards(): jnp.einsum('kgtf,kgfd->kgtd', query_feats, state, precision=precise)]
    add x35 -> x0, other arithmetic: 22.6 us -> none  [the longest x30 22.6 us: add_pair(): return (earlier[0] + later[0], earlier[1] + later[1])]
  transfers between devices with their start and end apart: 5 -> 3, of which waited for: 5 -> 2; matrix products, arithmetic and copies ran while one was open for 3% -> 2% of each run, Pallas kernels for 0% -> 0%
where the time goes in v1:
time: 156 us; the launch traced here: 155 us
  blocking collectives  41 us (26%)
  waiting for transfers between devices  40.9 us (26%)
  Pallas kernels  33.1 us (21%)
  starting transfers between devices  16.1 us (10%)
  between operations  14.7 us (9%)
  other arithmetic  5.03 us (3%)
  local copies, waits for them, and re-layouts  4.46 us (3%)
    psum x1, blocking collectives, head_shards(): squares = lax.psum(jnp.sum(grad * grad), ('ctx', 'head'))  41 us
    all_to_all x1, waiting for transfers between devices, head_shards(): x = lax.all_to_all(jnp.stack([q, k, v], axis=1), 'ctx', 0, 0)  34 us
    pallas_call x1, Pallas kernels, whole_head(): pl.pallas_call(head_kernel, out_shape=(jax.ShapeDtypeStruct((blocks, leng...  33.1 us
    all_to_all x1, starting transfers between devices, head_shards(): x = lax.all_to_all(jnp.stack([q, k, v], axis=1), 'ctx', 0, 0)  8.34 us
    all_to_all x1, starting transfers between devices, head_shards(): student = jnp.transpose(lax.all_to_all(mix, 'ctx', 0, 0), (1, 0, 2))  7.72 us
    all_gather x1, waiting for transfers between devices, head_shards(): gradients = lax.all_gather(grad, 'ctx', axis=0)  6.83 us
  transfers between devices with their start and end apart: 3, of which 2 were waited for; matrix products, arithmetic and copies ran while one was open for 2% of the time, Pallas kernels for 0%

profile of v1, /device:TPU:0, one launch (start us, length us, event | category | flops | bytes accessed | tf_op | source)
XLA Modules:
  0.0 155.2 jit_solution(7244859500410651377)
XLA Ops:
  7.2 0.0 copy-start
  7.2 1.0 copy.8
  8.2 0.9 copy.7
  9.1 1.2 copy.11
  10.3 0.1 broadcast_in_dim.7
  10.4 0.1 broadcast_in_dim.6
  10.5 1.3 pad_maximum_fusion
  11.8 8.3 %all-to-all-start = ((bf16[16,3,128,128]{3,2,1,0:T(8,128)(2,1)}), bf16[16,3,128,128]{3,2,1,0:T(8,128)(2,1)S(1)}, u32[]{:S(2)}, u32[]{:S(2)}) async-start(bf16[16,3,128,128]{3,2,1,0:T(8,128)(2,1)} %pad_maximum_fusion), calls=%async_computation | async-start | bytes 3145728 | tf_op jit(solution)/shard_map/all_to_all | solution.py:473
  20.2 0.0 all-gather.3.cloned.1.call-start
  20.2 0.0 copy-done
  20.3 34.0 %all-to-all-done.x_ref = bf16[16,3,128,128]{3,2,1,0:T(8,128)(2,1)S(1)} async-done(((bf16[16,3,128,128]{3,2,1,0:T(8,128)(2,1)}), bf16[16,3,128,128]{3,2,1,0:T(8,128)(2,1)S(1)}, u32[]{:S(2)}, u32[]{:S(2)}) %all-to-all-start) | async-done | bytes 1572896 | tf_op jit(solution)/shard_map/all_to_all | solution.py:473
  54.3 33.1 %shard_map.59 = (bf16[16,128,128]{2,1,0:T(8,128)(2,1)}, f32[128,128]{1,0:T(8,128)}) custom-call(bf16[16,3,128,128]{3,2,1,0:T(8,128)(2,1)S(1)} %all-to-all-done.x_ref, f32[128,128]{1,0:T(8,128)S(1)} %dynamic-slice_bitcast_fusion.w_ref), custom_call_target="tpu_custom_call" | custom-call | tf_op jit(solution)/shard_map/pallas_call | solution.py:438
  87.4 0.0 all-gather.3.cloned.1.call-update
  87.4 7.7 %all-to-all-start.1 = ((bf16[16,128,128]{2,1,0:T(8,128)(2,1)}), bf16[16,128,128]{2,1,0:T(8,128)(2,1)S(1)}, u32[]{:S(2)}, u32[]{:S(2)}) async-start(bf16[16,128,128]{2,1,0:T(8,128)(2,1)} %get-tuple-element.4), calls=%async_computation.1 | async-start | bytes 1048576 | tf_op jit(solution)/shard_map/all_to_all | solution.py:476
  95.1 1.4 multiply_reduce_fusion
  96.5 41.0 %psum.7 = f32[]{:T(128)} all-reduce(f32[]{:T(128)} %multiply_reduce_fusion), channel_id=1, replica_groups=mesh['ctx'=16,'head'=2] {'ctx','head'}, use_global_device_ids=true, to_apply=%region_1.2 | all-reduce | flops 1 | bytes 8 | tf_op jit(solution)/shard_map/psum | solution.py:477
  138.1 0.0 all-to-all-done.1
  138.2 1.1 copy.9
  139.3 6.8 %all-gather.3.cloned.1.call-done = f32[2048,128]{1,0:T(8,128)} async-done(((f32[128,128]{1,0:T(8,128)}), f32[2048,128]{1,0:T(8,128)}) %all-gather.3.cloned.1.call-update) | async-done | bytes 1048592 | tf_op jit(solution)/shard_map/all_gather | solution.py:478
  146.1 2.3 %broadcast_divide_fusion = f32[2048,128]{1,0:T(8,128)} fusion(f32[2048,128]{1,0:T(8,128)} %all-gather.3.cloned.1.call-done, f32[]{:T(128)S(6)} %sqrt.3), kind=kLoop, calls=%fused_computation.2 | loop fusion | flops 262144 | bytes 2097156 | tf_op jit(solution)/shard_map/div | solution.py:480
  (1 shorter events, 0.0 us)
Async XLA Ops:
  7.2 13.1 %copy-start = (f32[16,128,128]{2,1,0:T(8,128)S(1)}, f32[16,128,128]{2,1,0:T(8,128)}, u32[]{:S(2)}) copy-start(f32[16,128,128]{2,1,0:T(8,128)} %param.7) | copy-start | bytes 3145732
  11.8 42.4 %all-to-all-start = ((bf16[16,3,128,128]{3,2,1,0:T(8,128)(2,1)}), bf16[16,3,128,128]{3,2,1,0:T(8,128)(2,1)S(1)}, u32[]{:S(2)}, u32[]{:S(2)}) async-start(bf16[16,3,128,128]{3,2,1,0:T(8,128)(2,1)} %pad_maximum_fusion), calls=%async_computation | async-start | bytes 3145728 | tf_op jit(solution)/shard_map/all_to_all | solution.py:473
  20.2 125.9 %all-gather.3.cloned.1.call-start = ((), (), s32[]{:S(2)}) async-start(), calls=%async_computation.2 | async-start | bytes 1114112 | tf_op jit(solution)/shard_map/all_gather | solution.py:478
  87.4 50.8 %all-to-all-start.1 = ((bf16[16,128,128]{2,1,0:T(8,128)(2,1)}), bf16[16,128,128]{2,1,0:T(8,128)(2,1)S(1)}, u32[]{:S(2)}, u32[]{:S(2)}) async-start(bf16[16,128,128]{2,1,0:T(8,128)(2,1)} %get-tuple-element.4), calls=%async_computation.1 | async-start | bytes 1048576 | tf_op jit(solution)/shard_map/all_to_all | solution.py:476
Sparse Core Ops, SparseCore 0:
  87.5 58.5 all-gather.2

commit v2 on v1

--- a/solution.py
+++ b/solution.py
@@ -269,15 +269,132 @@
     return e / half_sum(e, halves)
 
 
+def remote(src, dst, send_sem, recv_sem, **where):
+    return pltpu.make_async_remote_copy(
+        src_ref=src,
+        dst_ref=dst,
+        send_sem=send_sem,
+        recv_sem=recv_sem,
+        device_id=where,
+        device_id_type=pl.DeviceIdType.MESH,
+    )
+
+
+def each(count, body):
+    def step(index, carry):
+        body(index)
+        return carry
+
+    lax.fori_loop(0, count, step, 0)
+
+
 def head_kernel(
-    x_ref, w_ref, student_ref, grad_ref,
+    qt_ref, kvt_ref, w_ref, student_ref, update_ref,
+    q_all, kv_all, mix_ref, gat_ref, sq_ref,
     score_ref, kfeat_ref, gstate_ref, gnorm_ref, state_ref, norm_ref, last_ref, lastn_ref,
     wq_ref, wk_ref, acc_ref, peak_ref, total_ref, gq_ref, gk_ref,
+    q_send, q_recv, kv_send, kv_recv, kv_relay, local_sem, st_send, st_recv,
+    g_send, g_relay, g_recv, sq_send, sq_recv,
 ):
-    blocks, _, length, width = x_ref.shape
+    blocks, length, width = qt_ref.shape
+    planes = kvt_ref.shape[0]
+    group = blocks // planes
+    me, side = lax.axis_index("ctx"), lax.axis_index("head")
+    plane, spot = me // group, me % group
     features = w_ref.shape[1] // 2
     rows = 2 * length
     steps = blocks // 2
+
+    barrier = pltpu.get_barrier_semaphore()
+
+    def greet(t):
+        @pl.when(t != me)
+        def _():
+            pl.semaphore_signal(
+                barrier, inc=1, device_id={"ctx": t}, device_id_type=pl.DeviceIdType.MESH
+            )
+
+    each(blocks, greet)
+    pl.semaphore_signal(
+        barrier, inc=1, device_id={"head": 1 - side}, device_id_type=pl.DeviceIdType.MESH
+    )
+    pl.semaphore_wait(barrier, blocks)
+
+    def kv_column(g):
+        return remote(
+            kvt_ref.at[g], kv_all.at[me], kv_send.at[g], kv_recv.at[me], ctx=g * group + spot
+        )
+
+    def kv_own(r):
+        return remote(
+            kvt_ref.at[plane], kv_all.at[me], kv_relay.at[plane, r], kv_recv.at[me],
+            ctx=plane * group + r,
+        )
+
+    def kv_pass(z, r):
+        block = z * group + spot
+        return remote(
+            kv_all.at[block], kv_all.at[block], kv_relay.at[z, r], kv_recv.at[block],
+            ctx=plane * group + r,
+        )
+
+    def q_copy(t):
+        return remote(qt_ref.at[t], q_all.at[me], q_send.at[t], q_recv.at[me], ctx=t)
+
+    def q_arrival(b):
+        return remote(qt_ref.at[b], q_all.at[b], q_send.at[b], q_recv.at[b], ctx=b)
+
+    def kv_arrival(b):
+        return remote(
+            kv_all.at[b], kv_all.at[b], kv_send.at[0], kv_recv.at[b], ctx=b
+        )
+
+    def st_copy(b):
+        return remote(mix_ref.at[b], student_ref.at[me], st_send.at[b], st_recv.at[me], ctx=b)
+
+    def st_arrival(b):
+        return remote(mix_ref.at[b], student_ref.at[b], st_send.at[b], st_recv.at[b], ctx=b)
+
+    def g_column(part, z):
+        piece = gat_ref.at[me, part]
+        return remote(
+            piece, piece, g_send.at[part, z], g_recv.at[me, part], ctx=z * group + spot
+        )
+
+    def g_pass(part, z, r):
+        block = z * group + spot
+        piece = gat_ref.at[block, part]
+        return remote(
+            piece, piece, g_relay.at[part, z, r], g_recv.at[block, part], ctx=plane * group + r
+        )
+
+    def g_arrival(part, b):
+        piece = gat_ref.at[b, part]
+        return remote(piece, piece, g_send.at[part, 0], g_recv.at[b, part], ctx=b)
+
+    def planes_but_mine(body):
+        def one(z):
+            @pl.when(z != plane)
+            def _():
+                body(z)
+
+        each(planes, one)
+
+    def spots_but_mine(body):
+        def one(r):
+            @pl.when(r != spot)
+            def _():
+                body(r)
+
+        each(group, one)
+
+    planes_but_mine(lambda g: kv_column(g).start())
+    spots_but_mine(lambda r: kv_own(r).start())
+    own_kv = pltpu.make_async_copy(kvt_ref.at[plane], kv_all.at[me], local_sem.at[0])
+    own_q = pltpu.make_async_copy(qt_ref.at[me], q_all.at[me], local_sem.at[1])
+    own_kv.start()
+    own_q.start()
+    each(blocks - 1, lambda d: q_copy((me + d + 1) % blocks).start())
     scale = 1.0 / math.sqrt(width)
     lane = lax.broadcasted_iota(jnp.int32, (rows, 2 * features), 1)
     is_upper = lane < features
@@ -290,11 +407,52 @@
     wk_ref[...] = cat(split(cat([wk, -wk], 1), 3), 0)
     for ref in (state_ref, norm_ref, last_ref, lastn_ref, gq_ref, gk_ref):
         ref[...] = jnp.zeros_like(ref)
+    own_kv.wait()
+    own_q.wait()
+
+    def pass_on(z):
+        kv_arrival(z * group + spot).wait_recv()
+        spots_but_mine(lambda r: kv_pass(z, r).start())
+
+    planes_but_mine(pass_on)
 
     def load(part, i):
-        return x_ref[pl.ds(2 * i, 2), part].reshape(rows, width)
+        if part == 0:
+            return q_all[pl.ds(2 * i, 2)].reshape(rows, width)
+        return kv_all[pl.ds(2 * i, 2), part - 1].reshape(rows, width)
+
+    def arrived(b):
+        @pl.when(b != me)
+        def _():
+            q_arrival(b).wait_recv()
+
+        @pl.when(b % group != spot)
+        def _():
+            kv_arrival(b).wait_recv()
+
+    def send_student(b):
+        @pl.when(b != me)
+        def _():
+            st_copy(b).start()
+
+        @pl.when(b == me)
+        def _():
+            student_ref[me] = mix_ref[me]
+
+    def send_grad(part):
+        planes_but_mine(lambda z: g_column(part, z).start())
+        spots_but_mine(lambda r: g_pass(part, plane, r).start())
+
+    def relay_grad(part):
+        def one(z):
+            g_arrival(part, z * group + spot).wait_recv()
+            spots_but_mine(lambda r: g_pass(part, z, r).start())
+
+        planes_but_mine(one)
 
     def forward(i, carry):
+        arrived(2 * i)
+        arrived(2 * i + 1)
         q, k, v = load(0, i), load(1, i), load(2, i)
         acc_ref[...] = jnp.zeros_like(acc_ref)
         total_ref[...] = jnp.zeros_like(total_ref)
@@ -339,7 +497,7 @@
         p_prev, p_own = jnp.exp(prev - win_max), jnp.exp(own - win_max)
         win_den = jnp.sum(p_prev + p_own, axis=-1, keepdims=True)
         b_prev, b_own = p_prev.astype(bf16), p_own.astype(bf16)
-        v_before = x_ref[jnp.maximum(2 * i - 1, 0), 2]
+        v_before = kv_all[jnp.maximum(2 * i - 1, 0), 1]
         win_num = cat(
             [
                 mxu(cat([b_prev[:length], b_own[:length]], 1), cat([v_before, v[:length]], 0), NN),
@@ -373,7 +531,9 @@
         )
         den = win_den + decay * jnp.sum(qf * norm, axis=-1, keepdims=True)
         mix = (win_num + decay * far) / den
-        student_ref[pl.ds(2 * i, 2)] = mix.astype(bf16).reshape(2, length, width)
+        mix_ref[pl.ds(2 * i, 2)] = mix.astype(bf16).reshape(2, length, width)
+        send_student(2 * i)
+        send_student(2 * i + 1)
         mismatch = mix - teacher
         g_num = mismatch / den
         g_den = -jnp.sum(mismatch * mix, axis=-1, keepdims=True) / den
@@ -394,10 +554,12 @@
             + norm * g_den
         )
         d_q = qf * (g_qf - half_sum(qf * g_qf, halves))
-        gq_ref[...] += exact_by_wide(q, d_q, TN)
+        gq_ref[...] += wide_by_exact(d_q, q, TN)
         return carry
 
     lax.fori_loop(0, steps, forward, 0)
+    gat_ref[me, 0] = gq_ref[:features] - gq_ref[features:]
+    send_grad(0)
 
     for ref in (state_ref, norm_ref):
         ref[...] = jnp.zeros_like(ref)
@@ -418,32 +580,94 @@
             0,
         )
         d_k = kf * (g_kf - half_sum(kf * g_kf, halves))
-        gk_ref[...] += exact_by_wide(k, d_k, TN)
+        gk_ref[...] += wide_by_exact(d_k, k, TN)
         state_ref[...] = later_0 + gstate_ref[2 * i + 1]
         norm_ref[...] = later_n0 + gnorm_ref[2 * i + 1]
         return carry
 
-    lax.fori_loop(0, steps, backward, 0)
-    gq, gk = gq_ref[...], gk_ref[...]
-    grad_ref[...] = cat(
-        [gq[:, :features] - gq[:, features:], gk[:, :features] - gk[:, features:]], 1
-    )
-
-
-def whole_head(x, w):
-    blocks, _, length, width = x.shape
+    lax.fori_loop(0, steps // 2, backward, 0)
+    relay_grad(0)
+    lax.fori_loop(steps // 2, steps, backward, 0)
+    gat_ref[me, 1] = gk_ref[:features] - gk_ref[features:]
+    send_grad(1)
+    relay_grad(1)
+
+    def gathered(b):
+        @pl.when(b % group != spot)
+        def _():
+            g_arrival(0, b).wait_recv()
+            g_arrival(1, b).wait_recv()
+
+    each(blocks, gathered)
+    squares = jnp.zeros((8, width), f32)
+    for b in range(blocks):
+        piece = gat_ref[b].reshape(2 * features // 8, 8, width)
+        squares = squares + jnp.sum(piece * piece, axis=0)
+    sq_ref[0] = squares
+    swap = remote(sq_ref.at[0], sq_ref.at[1], sq_send.at[0], sq_recv.at[0], head=1 - side)
+    swap.start()
+
+    def turned(b):
+        update_ref[b] = gat_ref[b].reshape(2 * features, width).T
+
+    each(blocks, turned)
+
+    def settle(t):
+        @pl.when(t != me)
+        def _():
+            q_copy(t).wait_send()
+            st_copy(t).wait_send()
+            st_arrival(t).wait_recv()
+
+    each(blocks, settle)
+
+    def settle_plane(z):
+        @pl.when(z != plane)
+        def _():
+            kv_column(z).wait_send()
+            g_column(0, z).wait_send()
+            g_column(1, z).wait_send()
+
+        def one(r):
+            kv_pass(z, r).wait_send()
+            g_pass(0, z, r).wait_send()
+            g_pass(1, z, r).wait_send()
+
+        spots_but_mine(one)
+
+    each(planes, settle_plane)
+    swap.wait()
+    entries = 2 * blocks * width * 2 * features
+    total = jnp.sum(sq_ref[0] + sq_ref[1], keepdims=True)
+    inverse = 1.0 / jnp.sqrt(total / entries + 1e-06)
+
+    def scaled(b):
+        update_ref[b] = update_ref[b] * inverse
+
+    each(blocks, scaled)
+
+
+def whole_head(qt, kvt, w):
+    blocks, length, width = qt.shape
+    planes = kvt.shape[0]
+    group = blocks // planes
     double = w.shape[1]
     rows, steps = 2 * length, blocks // 2
-    vmem = pltpu.VMEM
+    vmem, dma = pltpu.VMEM, pltpu.SemaphoreType.DMA
     return pl.pallas_call(
         head_kernel,
         out_shape=(
             jax.ShapeDtypeStruct((blocks, length, width), bf16),
-            jax.ShapeDtypeStruct((width, double), f32),
+            jax.ShapeDtypeStruct((blocks, width, double), f32),
         ),
-        in_specs=[pl.BlockSpec(memory_space=vmem)] * 2,
+        in_specs=[pl.BlockSpec(memory_space=vmem)] * 3,
         out_specs=(pl.BlockSpec(memory_space=vmem),) * 2,
         scratch_shapes=[
+            vmem((blocks, length, width), bf16),
+            vmem((blocks, 2, length, width), bf16),
+            vmem((blocks, length, width), bf16),
+            vmem((blocks, 2, double // 2, width), f32),
+            vmem((2, 8, width), f32),
             vmem((steps, rows, rows), f32),
             vmem((steps, rows, double), f32),
             vmem((blocks, double, width), f32),
@@ -457,34 +681,40 @@
             vmem((rows, width), f32),
             vmem((rows, length), f32),
             vmem((rows, length), f32),
-            vmem((width, double), f32),
-            vmem((width, double), f32),
+            vmem((double, width), f32),
+            vmem((double, width), f32),
+            dma((blocks,)),
+            dma((blocks,)),
+            dma((planes,)),
+            dma((blocks,)),
+            dma((planes, group)),
+            dma((2,)),
+            dma((blocks,)),
+            dma((blocks,)),
+            dma((2, planes)),
+            dma((2, planes, group)),
+            dma((blocks, 2)),
+            dma((1,)),
+            dma((1,)),
         ],
-        compiler_params=pltpu.CompilerParams(vmem_limit_bytes=40 * 2**20),
-    )(x, w)
+        compiler_params=pltpu.CompilerParams(
+            vmem_limit_bytes=40 * 2**20, collective_id=0, has_side_effects=True
+        ),
+    )(qt, kvt, w)
 
 
 def head_shards(queries, keys, values, feature_weight):
-    block_len, head_count, head_width = queries.shape
-    group = head_count // keys.shape[1]
-    q = jnp.transpose(queries, (1, 0, 2))
-    k = jnp.repeat(jnp.transpose(keys, (1, 0, 2)), group, axis=0)
-    v = jnp.repeat(jnp.transpose(values, (1, 0, 2)), group, axis=0)
-    x = lax.all_to_all(jnp.stack([q, k, v], axis=1), "ctx", 0, 0)
+    qt = jnp.transpose(queries, (1, 0, 2))
+    kvt = jnp.transpose(jnp.stack([keys, values]), (2, 0, 1, 3))
     w = lax.dynamic_index_in_dim(feature_weight, lax.axis_index("ctx"), 0, False)
-    mix, grad = whole_head(x, w)
-    student = jnp.transpose(lax.all_to_all(mix, "ctx", 0, 0), (1, 0, 2))
-    squares = lax.psum(jnp.sum(grad * grad), ("ctx", "head"))
-    gradients = lax.all_gather(grad, "ctx", axis=0)
-    entry_count = gradients.size * lax.axis_size("head")
-    update = gradients / jnp.sqrt(squares / entry_count + 1e-06)
-    return (student, update)
+    student, update = whole_head(qt, kvt, w)
+    return (jnp.transpose(student, (1, 0, 2)), update)
 
 
 def shards(queries, keys, values, feature_weight):
     count = lax.axis_size("ctx")
     width = queries.shape[2]
-    fits = queries.shape[1] == count and count % 2 == 0 and count * queries.shape[0] <= 4096
+    fits = queries.shape[1] == count and lax.axis_size("head") == 2 and count % 2 == 0 and count * queries.shape[0] <= 4096
     fits = fits and queries.shape[0] == width and feature_weight.shape[2] == width
     body = head_shards if fits else general_shards
     return body(queries, keys, values, feature_weight)

time: 156 us -> 75.3 us (0.48)
  blocking collectives: 41 us -> 0 us
  waiting for transfers between devices: 40.9 us -> 0 us
  Pallas kernels: 33.1 us -> 69.9 us
  starting transfers between devices: 16.1 us -> 0 us
  between operations: 14.7 us -> 0.68 us
  other arithmetic: 5.03 us -> 0.03 us
    psum x1 -> x0, blocking collectives: 41 us -> none  [head_shards(): squares = lax.psum(jnp.sum(grad * grad), ('ctx', 'head'))]
    pallas_call x1, Pallas kernels: 33.1 us -> 69.9 us  [whole_head(): pl.pallas_call(head_kernel, out_shape=(jax.ShapeDtypeStruct((blocks, leng...]
    all_to_all x2 -> x0, waiting for transfers between devices: 34 us -> none  [the longest x1 34 us: head_shards(): x = lax.all_to_all(jnp.stack([q, k, v], axis=1), 'ctx', 0, 0)]
    all_to_all x2 -> x0, starting transfers between devices: 16.1 us -> none  [the longest x1 8.34 us: head_shards(): x = lax.all_to_all(jnp.stack([q, k, v], axis=1), 'ctx', 0, 0)]
    all_gather x1 -> x0, waiting for transfers between devices: 6.83 us -> none  [head_shards(): gradients = lax.all_gather(grad, 'ctx', axis=0)]
    div x1 -> x0, other arithmetic: 2.27 us -> none  [head_shards(): update = gradients / jnp.sqrt(squares / entry_count + 1e-06)]
    transpose x2 -> x0, local copies, waits for them, and re-layouts: 1.94 us -> none  [the longest x1 1.01 us: head_shards(): v = jnp.repeat(jnp.transpose(values, (1, 0, 2)), group, axis=0)]
    unnamed x4 -> x9, local copies, waits for them, and re-layouts: 2.32 us -> 3.52 us
  transfers between devices with their start and end apart: 3 -> 0, of which waited for: 2 -> 0; matrix products, arithmetic and copies ran while one was open for 2% -> 0% of each run, Pallas kernels for 0% -> 0%
where the time goes in v2:
time: 75.3 us; the launch traced here: 75.1 us
  Pallas kernels  69.9 us (93%)
  local copies, waits for them, and re-layouts  4.52 us (6%)
    pallas_call x1, Pallas kernels, whole_head(): pl.pallas_call(head_kernel, out_shape=(jax.ShapeDtypeStruct((blocks, leng...  69.9 us
    unnamed x9, local copies, waits for them, and re-layouts  3.52 us

profile of v2, /device:TPU:0, one launch (start us, length us, event | category | flops | bytes accessed | tf_op | source)
XLA Modules:
  0.0 75.1 jit_solution(3038516979154462073)
XLA Ops:
  0.6 0.0 copy-start
  0.6 0.0 copy-start.2
  0.7 1.2 %copy-done = f32[16,128,128]{2,1,0:T(8,128)S(1)} copy-done((f32[16,128,128]{2,1,0:T(8,128)S(1)}, f32[16,128,128]{2,1,0:T(8,128)}, u32[]{:S(2)}) %copy-start) | copy-done | bytes 1048600
  1.9 0.0 copy-done.2
  1.9 0.0 copy-start.1
  1.9 1.0 %copy_bitcast_fusion.1 = (bf16[1,128,4,128]{3,1,0,2:T(8,128)(2,1)S(1)}, bf16[1,128,4,128]{3,1,0,2:T(8,128)(2,1)S(1)}) fusion(bf16[128,4,128]{2,1,0:T(4,128)(2,1)S(1)} %copy-done.2, bf16[128,4,128]{2,1,0:T(4,128)(2,1)} %param.5), kind=kLoop, calls=%fused_computation.2 | loop fusion | bytes 524288 | tf_op jit(solution)/shard_map/stack | solution.py:708
  2.9 0.1 copy-done.1
  3.0 0.1 copy.13
  3.1 69.9 %shard_map.59 = (bf16[16,128,128]{2,1,0:T(8,128)(2,1)S(1)}, f32[16,128,128]{2,1,0:T(8,128)S(1)}) custom-call(bf16[16,128,128]{2,1,0:T(8,128)(2,1)S(1)} %bitcast.12, bf16[4,2,128,128]{3,2,1,0:T(8,128)(2,1)S(1)} %maximum_bitcast_fusion.kvt_ref, f32[128,128]{1,0:T(8,128)S(1)} %dynamic-slice_bitcast_fusion.w_ref), custom_call_target="tpu_custom_call" | custom-call | tf_op jit(solution)/shard_map/pallas_call | solution.py:657
  73.0 1.1 %copy.9 = bf16[128,16,128]{2,1,0:T(8,128)(2,1)} copy(bf16[128,16,128]{2,0,1:T(8,128)(2,1)S(1)} %bitcast.13) | data formatting | bytes 1048576
  74.2 1.0 %copy.15 = f32[16,128,128]{2,1,0:T(8,128)} copy(f32[16,128,128]{2,1,0:T(8,128)S(1)} %get-tuple-element.13) | data formatting | bytes 2097152
  (2 shorter events, 0.0 us)
Async XLA Ops:
  0.6 1.2 %copy-start = (f32[16,128,128]{2,1,0:T(8,128)S(1)}, f32[16,128,128]{2,1,0:T(8,128)}, u32[]{:S(2)}) copy-start(f32[16,128,128]{2,1,0:T(8,128)} %param.7) | copy-start | bytes 3145732
  0.6 1.2 %copy-start.2 = (bf16[128,4,128]{2,1,0:T(4,128)(2,1)S(1)}, bf16[128,4,128]{2,1,0:T(4,128)(2,1)}, u32[]{:S(2)}) copy-start(bf16[128,4,128]{2,1,0:T(4,128)(2,1)} %param.6) | copy-start | bytes 393220
  1.9 1.1 %copy-start.1 = (bf16[128,16,128]{2,1,0:T(8,128)(2,1)S(1)}, bf16[128,16,128]{2,1,0:T(8,128)(2,1)}, u32[]{:S(2)}) copy-start(bf16[128,16,128]{2,1,0:T(8,128)(2,1)} %param.4) | copy-start | bytes 1572868

commit v3 on v2

--- a/solution.py
+++ b/solution.py
@@ -290,8 +290,8 @@
 
 def head_kernel(
     qt_ref, kvt_ref, w_ref, student_ref, update_ref,
-    q_all, kv_all, mix_ref, gat_ref, sq_ref,
-    score_ref, kfeat_ref, gstate_ref, gnorm_ref, state_ref, norm_ref, last_ref, lastn_ref,
+    q_all, kv_all, mix_ref, gat_ref, gat_key_ref, sq_ref, own_ref, sum_ref, pre_ref, pre_norm_ref,
+    score_ref, kfeat_ref, gstate_ref, gnorm_ref, state_ref, norm_ref,
     wq_ref, wk_ref, acc_ref, peak_ref, total_ref, gq_ref, gk_ref,
     q_send, q_recv, kv_send, kv_recv, kv_relay, local_sem, st_send, st_recv,
     g_send, g_relay, g_recv, sq_send, sq_recv,
@@ -305,6 +305,7 @@
     rows = 2 * length
     steps = blocks // 2
 
+    gats = (gat_ref, gat_key_ref)
     barrier = pltpu.get_barrier_semaphore()
 
     def greet(t):
@@ -356,20 +357,20 @@
         return remote(mix_ref.at[b], student_ref.at[b], st_send.at[b], st_recv.at[b], ctx=b)
 
     def g_column(part, z):
-        piece = gat_ref.at[me, part]
+        piece = gats[part].at[me]
         return remote(
             piece, piece, g_send.at[part, z], g_recv.at[me, part], ctx=z * group + spot
         )
 
     def g_pass(part, z, r):
         block = z * group + spot
-        piece = gat_ref.at[block, part]
+        piece = gats[part].at[block]
         return remote(
             piece, piece, g_relay.at[part, z, r], g_recv.at[block, part], ctx=plane * group + r
         )
 
     def g_arrival(part, b):
-        piece = gat_ref.at[b, part]
+        piece = gats[part].at[b]
         return remote(piece, piece, g_send.at[part, 0], g_recv.at[b, part], ctx=b)
 
     def planes_but_mine(body):
@@ -394,7 +395,6 @@
     own_q = pltpu.make_async_copy(qt_ref.at[me], q_all.at[me], local_sem.at[1])
     own_kv.start()
     own_q.start()
-    each(blocks - 1, lambda d: q_copy((me + d + 1) % blocks).start())
     scale = 1.0 / math.sqrt(width)
     lane = lax.broadcasted_iota(jnp.int32, (rows, 2 * features), 1)
     is_upper = lane < features
@@ -405,7 +405,7 @@
     wq, wk = w[:, :features], w[:, features:]
     wq_ref[...] = cat(split(cat([wq, -wq], 1), 3), 0)
     wk_ref[...] = cat(split(cat([wk, -wk], 1), 3), 0)
-    for ref in (state_ref, norm_ref, last_ref, lastn_ref, gq_ref, gk_ref):
+    for ref in (state_ref, norm_ref, gq_ref, gk_ref):
         ref[...] = jnp.zeros_like(ref)
     own_kv.wait()
     own_q.wait()
@@ -414,18 +414,18 @@
         kv_arrival(z * group + spot).wait_recv()
         spots_but_mine(lambda r: kv_pass(z, r).start())
 
-    planes_but_mine(pass_on)
 
     def load(part, i):
         if part == 0:
             return q_all[pl.ds(2 * i, 2)].reshape(rows, width)
         return kv_all[pl.ds(2 * i, 2), part - 1].reshape(rows, width)
 
-    def arrived(b):
+    def q_arrived(b):
         @pl.when(b != me)
         def _():
             q_arrival(b).wait_recv()
 
+    def kv_arrived(b):
         @pl.when(b % group != spot)
         def _():
             kv_arrival(b).wait_recv()
@@ -450,45 +450,85 @@
 
         planes_but_mine(one)
 
-    def forward(i, carry):
-        arrived(2 * i)
-        arrived(2 * i + 1)
-        q, k, v = load(0, i), load(1, i), load(2, i)
+    def key_side(i):
+        kv_arrived(2 * i)
+        kv_arrived(2 * i + 1)
+        k, v = load(1, i), load(2, i)
+        kf = half_softmax(mxu(cat([k, k, k], 1), wk_ref[...], NN), is_upper, halves)
+        kfeat_ref[i] = kf
+        own_ref[2 * i] = wide_by_exact(kf[:length], v[:length], TN)
+        own_ref[2 * i + 1] = wide_by_exact(kf[length:], v[length:], TN)
+        sum_ref[2 * i] = jnp.sum(kf[:length], axis=0, keepdims=True)
+        sum_ref[2 * i + 1] = jnp.sum(kf[length:], axis=0, keepdims=True)
+
+    def stage(dz):
+        @pl.when(dz < planes - 1)
+        def _():
+            pass_on((plane + dz + 1) % planes)
+
+        def push(u):
+            d = dz * group + u
+
+            @pl.when(d > 0)
+            def _():
+                q_copy((me + blocks - d) % blocks).start()
+
+        each(group, push)
+        half = group // 2
+        each(half, lambda u: key_side((plane + dz) % planes * half + u))
+
+    each(planes, stage)
+    for b in range(2):
+        pre_ref[b] = jnp.zeros_like(pre_ref[b])
+        pre_norm_ref[b] = jnp.zeros_like(pre_norm_ref[b])
+
+    def prefix(b):
+        pre_ref[b + 2] = pre_ref[b + 1] + own_ref[b]
+        pre_norm_ref[b + 2] = pre_norm_ref[b + 1] + sum_ref[b]
+
+    each(blocks - 2, prefix)
+
+    def forward(turn, carry):
+        i = (me // 2 + turn) % steps
+        q_arrived(2 * i)
+        q_arrived(2 * i + 1)
+        q, v = load(0, i), load(2, i)
         acc_ref[...] = jnp.zeros_like(acc_ref)
         total_ref[...] = jnp.zeros_like(total_ref)
         peak_ref[...] = jnp.full(peak_ref.shape, big_negative, f32)
 
-        def score(j, carry):
-            s = mxu(q, load(1, j), NT) * scale
-            score_ref[j] = s
+        def pair_of(part, j):
+            return cat([load(part, 2 * j), load(part, 2 * j + 1)], 0)
+
+        def keep(j, s):
+            score_ref[2 * j] = s[:, :rows]
+            score_ref[2 * j + 1] = s[:, rows:]
+            top = jnp.maximum(s[:, :rows], s[:, rows:])
             peak_ref[...] = jnp.maximum(
-                peak_ref[...], jnp.maximum(s[:, :length], s[:, length:])
+                peak_ref[...], jnp.maximum(top[:, :length], top[:, length:])
             )
-            return carry
-
-        lax.fori_loop(0, i, score, 0)
-        s = mxu(q, k, NT) * scale
-        causal = lax.broadcasted_iota(jnp.int32, (rows, rows), 1) <= lax.broadcasted_iota(
-            jnp.int32, (rows, rows), 0
-        )
-        s = jnp.where(causal, s, big_negative)
-        score_ref[i] = s
-        row_max = jnp.max(
-            jnp.maximum(peak_ref[...], jnp.maximum(s[:, :length], s[:, length:])),
-            axis=-1,
-            keepdims=True,
-        )
-
-        def weigh(j, carry):
-            p = jnp.exp(score_ref[j] - row_max)
-            total_ref[...] += p[:, :length] + p[:, length:]
-            acc_ref[...] += mxu(p.astype(bf16), load(2, j), NN)
-            return carry
-
-        lax.fori_loop(0, i + 1, weigh, 0)
+
+        last = i // 2
+        each(last, lambda j: keep(j, mxu(q, pair_of(1, j), NT) * scale))
+        s = mxu(q, pair_of(1, last), NT) * scale
+        column = lax.broadcasted_iota(jnp.int32, (rows, 2 * rows), 1)
+        row = lax.broadcasted_iota(jnp.int32, (rows, 2 * rows), 0)
+        keep(last, jnp.where(column <= row + (i - 2 * last) * rows, s, big_negative))
+        row_max = jnp.max(peak_ref[...], axis=-1, keepdims=True)
+
+        def weigh(j):
+            p0 = jnp.exp(score_ref[2 * j] - row_max)
+            p1 = jnp.exp(score_ref[2 * j + 1] - row_max)
+            both = p0 + p1
+            total_ref[...] += both[:, :length] + both[:, length:]
+            p = cat([p0.astype(bf16), p1.astype(bf16)], 1)
+            acc_ref[...] += mxu(p, pair_of(2, j), NN)
+
+        each(last + 1, weigh)
         teacher = acc_ref[...] / jnp.sum(total_ref[...], axis=-1, keepdims=True)
 
         before = jnp.maximum(i - 1, 0)
+        s = score_ref[i]
         prev_top = score_ref[before, :length, length:]
         prev_top = jnp.where(i > 0, prev_top, big_negative)
         prev = cat([prev_top, s[length:, :length]], 0)
@@ -507,16 +547,8 @@
         )
 
         qf = half_softmax(mxu(cat([q, q, q], 1), wq_ref[...], NN), is_upper, halves)
-        kf = half_softmax(mxu(cat([k, k, k], 1), wk_ref[...], NN), is_upper, halves)
-        kfeat_ref[i] = kf
-        own_0 = wide_by_exact(kf[:length], v[:length], TN)
-        own_1 = wide_by_exact(kf[length:], v[length:], TN)
-        sum_0 = jnp.sum(kf[:length], axis=0, keepdims=True)
-        sum_1 = jnp.sum(kf[length:], axis=0, keepdims=True)
-        state_0, norm_0 = state_ref[...], norm_ref[...]
-        state_1, norm_1 = state_0 + last_ref[...], norm_0 + lastn_ref[...]
-        state_ref[...], norm_ref[...] = state_1 + own_0, norm_1 + sum_0
-        last_ref[...], lastn_ref[...] = own_1, sum_1
+        state_0, norm_0 = pre_ref[2 * i], pre_norm_ref[2 * i]
+        state_1, norm_1 = pre_ref[2 * i + 1], pre_norm_ref[2 * i + 1]
 
         norm = cat(
             [
@@ -558,7 +590,7 @@
         return carry
 
     lax.fori_loop(0, steps, forward, 0)
-    gat_ref[me, 0] = gq_ref[:features] - gq_ref[features:]
+    gat_ref[me] = gq_ref[:features] - gq_ref[features:]
     send_grad(0)
 
     for ref in (state_ref, norm_ref):
@@ -588,7 +620,7 @@
     lax.fori_loop(0, steps // 2, backward, 0)
     relay_grad(0)
     lax.fori_loop(steps // 2, steps, backward, 0)
-    gat_ref[me, 1] = gk_ref[:features] - gk_ref[features:]
+    gat_key_ref[me] = (gk_ref[:features] - gk_ref[features:]).astype(bf16)
     send_grad(1)
     relay_grad(1)
 
@@ -601,14 +633,15 @@
     each(blocks, gathered)
     squares = jnp.zeros((8, width), f32)
     for b in range(blocks):
-        piece = gat_ref[b].reshape(2 * features // 8, 8, width)
+        piece = cat([gat_ref[b], gat_key_ref[b].astype(f32)], 0)
+        piece = piece.reshape(2 * features // 8, 8, width)
         squares = squares + jnp.sum(piece * piece, axis=0)
     sq_ref[0] = squares
     swap = remote(sq_ref.at[0], sq_ref.at[1], sq_send.at[0], sq_recv.at[0], head=1 - side)
     swap.start()
 
     def turned(b):
-        update_ref[b] = gat_ref[b].reshape(2 * features, width).T
+        update_ref[b] = cat([gat_ref[b], gat_key_ref[b].astype(f32)], 0).T
 
     each(blocks, turned)
 
@@ -666,14 +699,17 @@
             vmem((blocks, length, width), bf16),
             vmem((blocks, 2, length, width), bf16),
             vmem((blocks, length, width), bf16),
-            vmem((blocks, 2, double // 2, width), f32),
+            vmem((blocks, double // 2, width), f32),
+            vmem((blocks, double // 2, width), bf16),
             vmem((2, 8, width), f32),
+            vmem((blocks, double, width), f32),
+            vmem((blocks, 1, double), f32),
+            vmem((blocks, double, width), f32),
+            vmem((blocks, 1, double), f32),
             vmem((steps, rows, rows), f32),
             vmem((steps, rows, double), f32),
             vmem((blocks, double, width), f32),
             vmem((blocks, 1, double), f32),
-            vmem((double, width), f32),
-            vmem((1, double), f32),
             vmem((double, width), f32),
             vmem((1, double), f32),
             vmem((3 * width, double), bf16),
@@ -714,8 +750,8 @@
 def shards(queries, keys, values, feature_weight):
     count = lax.axis_size("ctx")
     width = queries.shape[2]
-    fits = queries.shape[1] == count and lax.axis_size("head") == 2 and count % 2 == 0 and count * queries.shape[0] <= 4096
-    fits = fits and queries.shape[0] == width and feature_weight.shape[2] == width
+    fits = queries.shape[1] == count and lax.axis_size("head") == 2 and count % 4 == 0 and count * queries.shape[0] <= 4096
+    fits = fits and queries.shape[1] // keys.shape[1] % 2 == 0 and queries.shape[0] == width and feature_weight.shape[2] == width
     body = head_shards if fits else general_shards
     return body(queries, keys, values, feature_weight)
 

time: 75.3 us -> 73.6 us (0.977)
  Pallas kernels: 69.9 us -> 68.2 us
    pallas_call x1, Pallas kernels: 69.9 us -> 68.2 us  [whole_head(): pl.pallas_call(head_kernel, out_shape=(jax.ShapeDtypeStruct((blocks, leng...]
where the time goes in v3:
time: 73.6 us; the launch traced here: 73.4 us
  Pallas kernels  68.2 us (93%)
  local copies, waits for them, and re-layouts  4.52 us (6%)
    pallas_call x1, Pallas kernels, whole_head(): pl.pallas_call(head_kernel, out_shape=(jax.ShapeDtypeStruct((blocks, leng...  68.2 us
    unnamed x9, local copies, waits for them, and re-layouts  3.52 us

profile of v3, /device:TPU:0, one launch (start us, length us, event | category | flops | bytes accessed | tf_op | source)
XLA Modules:
  0.0 73.4 jit_solution(4623520009328768590)
XLA Ops:
  0.6 0.0 copy-start
  0.6 0.0 copy-start.2
  0.7 1.2 %copy-done = f32[16,128,128]{2,1,0:T(8,128)S(1)} copy-done((f32[16,128,128]{2,1,0:T(8,128)S(1)}, f32[16,128,128]{2,1,0:T(8,128)}, u32[]{:S(2)}) %copy-start) | copy-done | bytes 1048600
  1.9 0.0 copy-done.2
  1.9 0.0 copy-start.1
  1.9 1.0 %copy_bitcast_fusion.1 = (bf16[1,128,4,128]{3,1,0,2:T(8,128)(2,1)S(1)}, bf16[1,128,4,128]{3,1,0,2:T(8,128)(2,1)S(1)}) fusion(bf16[128,4,128]{2,1,0:T(4,128)(2,1)S(1)} %copy-done.2, bf16[128,4,128]{2,1,0:T(4,128)(2,1)} %param.5), kind=kLoop, calls=%fused_computation.2 | loop fusion | bytes 524288 | tf_op jit(solution)/shard_map/stack | solution.py:744
  2.9 0.1 copy-done.1
  3.0 0.1 copy.13
  3.1 68.2 %shard_map.59 = (bf16[16,128,128]{2,1,0:T(8,128)(2,1)S(1)}, f32[16,128,128]{2,1,0:T(8,128)S(1)}) custom-call(bf16[16,128,128]{2,1,0:T(8,128)(2,1)S(1)} %bitcast.12, bf16[4,2,128,128]{3,2,1,0:T(8,128)(2,1)S(1)} %maximum_bitcast_fusion.kvt_ref, f32[128,128]{1,0:T(8,128)S(1)} %dynamic-slice_bitcast_fusion.w_ref), custom_call_target="tpu_custom_call" | custom-call | tf_op jit(solution)/shard_map/pallas_call | solution.py:690
  71.3 1.1 %copy.9 = bf16[128,16,128]{2,1,0:T(8,128)(2,1)} copy(bf16[128,16,128]{2,0,1:T(8,128)(2,1)S(1)} %bitcast.13) | data formatting | bytes 1048576
  72.5 1.0 %copy.15 = f32[16,128,128]{2,1,0:T(8,128)} copy(f32[16,128,128]{2,1,0:T(8,128)S(1)} %get-tuple-element.13) | data formatting | bytes 2097152
  (2 shorter events, 0.0 us)
Async XLA Ops:
  0.6 1.2 %copy-start = (f32[16,128,128]{2,1,0:T(8,128)S(1)}, f32[16,128,128]{2,1,0:T(8,128)}, u32[]{:S(2)}) copy-start(f32[16,128,128]{2,1,0:T(8,128)} %param.7) | copy-start | bytes 3145732
  0.6 1.2 %copy-start.2 = (bf16[128,4,128]{2,1,0:T(4,128)(2,1)S(1)}, bf16[128,4,128]{2,1,0:T(4,128)(2,1)}, u32[]{:S(2)}) copy-start(bf16[128,4,128]{2,1,0:T(4,128)(2,1)} %param.6) | copy-start | bytes 393220
  1.9 1.1 %copy-start.1 = (bf16[128,16,128]{2,1,0:T(8,128)(2,1)S(1)}, bf16[128,16,128]{2,1,0:T(8,128)(2,1)}, u32[]{:S(2)}) copy-start(bf16[128,16,128]{2,1,0:T(8,128)(2,1)} %param.4) | copy-start | bytes 1572868

commit v4 on v3

--- a/solution.py
+++ b/solution.py
@@ -461,19 +461,17 @@
         sum_ref[2 * i] = jnp.sum(kf[:length], axis=0, keepdims=True)
         sum_ref[2 * i + 1] = jnp.sum(kf[length:], axis=0, keepdims=True)
 
+    def push(d):
+        q_copy((me + 2 * blocks - 1 - d) % blocks).start()
+
+    each(blocks - 1, push)
+
+    def relay_first(dz):
+        pass_on((plane + dz + 1) % planes)
+
+    each(planes - 1, relay_first)
+
     def stage(dz):
-        @pl.when(dz < planes - 1)
-        def _():
-            pass_on((plane + dz + 1) % planes)
-
-        def push(u):
-            d = dz * group + u
-
-            @pl.when(d > 0)
-            def _():
-                q_copy((me + blocks - d) % blocks).start()
-
-        each(group, push)
         half = group // 2
         each(half, lambda u: key_side((plane + dz) % planes * half + u))
 
@@ -590,7 +588,7 @@
         return carry
 
     lax.fori_loop(0, steps, forward, 0)
-    gat_ref[me] = gq_ref[:features] - gq_ref[features:]
+    gat_ref[me] = (gq_ref[:features] - gq_ref[features:]).astype(bf16)
     send_grad(0)
 
     for ref in (state_ref, norm_ref):
@@ -633,7 +631,7 @@
     each(blocks, gathered)
     squares = jnp.zeros((8, width), f32)
     for b in range(blocks):
-        piece = cat([gat_ref[b], gat_key_ref[b].astype(f32)], 0)
+        piece = cat([gat_ref[b], gat_key_ref[b]], 0).astype(f32)
         piece = piece.reshape(2 * features // 8, 8, width)
         squares = squares + jnp.sum(piece * piece, axis=0)
     sq_ref[0] = squares
@@ -641,7 +639,7 @@
     swap.start()
 
     def turned(b):
-        update_ref[b] = cat([gat_ref[b], gat_key_ref[b].astype(f32)], 0).T
+        update_ref[b] = cat([gat_ref[b], gat_key_ref[b]], 0).astype(f32).T
 
     each(blocks, turned)
 
@@ -699,7 +697,7 @@
             vmem((blocks, length, width), bf16),
             vmem((blocks, 2, length, width), bf16),
             vmem((blocks, length, width), bf16),
-            vmem((blocks, double // 2, width), f32),
+            vmem((blocks, double // 2, width), bf16),
             vmem((blocks, double // 2, width), bf16),
             vmem((2, 8, width), f32),
             vmem((blocks, double, width), f32),

time: 73.6 us -> 71.8 us (0.976)
  Pallas kernels: 68.2 us -> 66.4 us
    pallas_call x1, Pallas kernels: 68.2 us -> 66.4 us  [whole_head(): pl.pallas_call(head_kernel, out_shape=(jax.ShapeDtypeStruct((blocks, leng...]
where the time goes in v4:
time: 71.8 us; the launch traced here: 71.6 us
  Pallas kernels  66.4 us (92%)
  local copies, waits for them, and re-layouts  4.52 us (6%)
    pallas_call x1, Pallas kernels, whole_head(): pl.pallas_call(head_kernel, out_shape=(jax.ShapeDtypeStruct((blocks, leng...  66.4 us
    unnamed x9, local copies, waits for them, and re-layouts  3.52 us

profile of v4, /device:TPU:0, one launch (start us, length us, event | category | flops | bytes accessed | tf_op | source)
XLA Modules:
  0.0 71.6 jit_solution(4833112433743762689)
XLA Ops:
  0.6 0.0 copy-start
  0.6 0.0 copy-start.2
  0.7 1.2 %copy-done = f32[16,128,128]{2,1,0:T(8,128)S(1)} copy-done((f32[16,128,128]{2,1,0:T(8,128)S(1)}, f32[16,128,128]{2,1,0:T(8,128)}, u32[]{:S(2)}) %copy-start) | copy-done | bytes 1048600
  1.9 0.0 copy-done.2
  1.9 0.0 copy-start.1
  1.9 1.0 %copy_bitcast_fusion.1 = (bf16[1,128,4,128]{3,1,0,2:T(8,128)(2,1)S(1)}, bf16[1,128,4,128]{3,1,0,2:T(8,128)(2,1)S(1)}) fusion(bf16[128,4,128]{2,1,0:T(4,128)(2,1)S(1)} %copy-done.2, bf16[128,4,128]{2,1,0:T(4,128)(2,1)} %param.5), kind=kLoop, calls=%fused_computation.2 | loop fusion | bytes 524288 | tf_op jit(solution)/shard_map/stack | solution.py:742
  2.9 0.1 copy-done.1
  3.0 0.1 copy.13
  3.1 66.4 %shard_map.59 = (bf16[16,128,128]{2,1,0:T(8,128)(2,1)S(1)}, f32[16,128,128]{2,1,0:T(8,128)S(1)}) custom-call(bf16[16,128,128]{2,1,0:T(8,128)(2,1)S(1)} %bitcast.12, bf16[4,2,128,128]{3,2,1,0:T(8,128)(2,1)S(1)} %maximum_bitcast_fusion.kvt_ref, f32[128,128]{1,0:T(8,128)S(1)} %dynamic-slice_bitcast_fusion.w_ref), custom_call_target="tpu_custom_call" | custom-call | tf_op jit(solution)/shard_map/pallas_call | solution.py:688
  69.5 1.1 %copy.9 = bf16[128,16,128]{2,1,0:T(8,128)(2,1)} copy(bf16[128,16,128]{2,0,1:T(8,128)(2,1)S(1)} %bitcast.13) | data formatting | bytes 1048576
  70.7 1.0 %copy.15 = f32[16,128,128]{2,1,0:T(8,128)} copy(f32[16,128,128]{2,1,0:T(8,128)S(1)} %get-tuple-element.13) | data formatting | bytes 2097152
  (2 shorter events, 0.0 us)
Async XLA Ops:
  0.6 1.2 %copy-start = (f32[16,128,128]{2,1,0:T(8,128)S(1)}, f32[16,128,128]{2,1,0:T(8,128)}, u32[]{:S(2)}) copy-start(f32[16,128,128]{2,1,0:T(8,128)} %param.7) | copy-start | bytes 3145732
  0.6 1.2 %copy-start.2 = (bf16[128,4,128]{2,1,0:T(4,128)(2,1)S(1)}, bf16[128,4,128]{2,1,0:T(4,128)(2,1)}, u32[]{:S(2)}) copy-start(bf16[128,4,128]{2,1,0:T(4,128)(2,1)} %param.6) | copy-start | bytes 393220
  1.9 1.1 %copy-start.1 = (bf16[128,16,128]{2,1,0:T(8,128)(2,1)S(1)}, bf16[128,16,128]{2,1,0:T(8,128)(2,1)}, u32[]{:S(2)}) copy-start(bf16[128,16,128]{2,1,0:T(8,128)(2,1)} %param.4) | copy-start | bytes 1572868

commit v5 on v4

--- a/solution.py
+++ b/solution.py
@@ -615,11 +615,10 @@
         norm_ref[...] = later_n0 + gnorm_ref[2 * i + 1]
         return carry
 
-    lax.fori_loop(0, steps // 2, backward, 0)
-    relay_grad(0)
-    lax.fori_loop(steps // 2, steps, backward, 0)
+    lax.fori_loop(0, steps, backward, 0)
     gat_key_ref[me] = (gk_ref[:features] - gk_ref[features:]).astype(bf16)
     send_grad(1)
+    relay_grad(0)
     relay_grad(1)
 
     def gathered(b):

time: 71.8 us -> 70.8 us (0.986)
  Pallas kernels: 66.4 us -> 65.4 us
    pallas_call x1, Pallas kernels: 66.4 us -> 65.4 us  [whole_head(): pl.pallas_call(head_kernel, out_shape=(jax.ShapeDtypeStruct((blocks, leng...]
where the time goes in v5:
time: 70.8 us; the launch traced here: 70.7 us
  Pallas kernels  65.4 us (92%)
  local copies, waits for them, and re-layouts  4.52 us (6%)
    pallas_call x1, Pallas kernels, whole_head(): pl.pallas_call(head_kernel, out_shape=(jax.ShapeDtypeStruct((blocks, leng...  65.4 us
    unnamed x9, local copies, waits for them, and re-layouts  3.52 us

profile of v5, /device:TPU:0, one launch (start us, length us, event | category | flops | bytes accessed | tf_op | source)
XLA Modules:
  0.0 70.7 jit_solution(11952156818924180778)
XLA Ops:
  0.6 0.0 copy-start
  0.6 0.0 copy-start.2
  0.7 1.2 %copy-done = f32[16,128,128]{2,1,0:T(8,128)S(1)} copy-done((f32[16,128,128]{2,1,0:T(8,128)S(1)}, f32[16,128,128]{2,1,0:T(8,128)}, u32[]{:S(2)}) %copy-start) | copy-done | bytes 1048600
  1.9 0.0 copy-done.2
  1.9 0.0 copy-start.1
  1.9 1.0 %copy_bitcast_fusion.1 = (bf16[1,128,4,128]{3,1,0,2:T(8,128)(2,1)S(1)}, bf16[1,128,4,128]{3,1,0,2:T(8,128)(2,1)S(1)}) fusion(bf16[128,4,128]{2,1,0:T(4,128)(2,1)S(1)} %copy-done.2, bf16[128,4,128]{2,1,0:T(4,128)(2,1)} %param.5), kind=kLoop, calls=%fused_computation.2 | loop fusion | bytes 524288 | tf_op jit(solution)/shard_map/stack | solution.py:741
  2.9 0.1 copy-done.1
  3.0 0.1 copy.13
  3.1 65.4 %shard_map.59 = (bf16[16,128,128]{2,1,0:T(8,128)(2,1)S(1)}, f32[16,128,128]{2,1,0:T(8,128)S(1)}) custom-call(bf16[16,128,128]{2,1,0:T(8,128)(2,1)S(1)} %bitcast.12, bf16[4,2,128,128]{3,2,1,0:T(8,128)(2,1)S(1)} %maximum_bitcast_fusion.kvt_ref, f32[128,128]{1,0:T(8,128)S(1)} %dynamic-slice_bitcast_fusion.w_ref), custom_call_target="tpu_custom_call" | custom-call | tf_op jit(solution)/shard_map/pallas_call | solution.py:687
  68.6 1.1 %copy.9 = bf16[128,16,128]{2,1,0:T(8,128)(2,1)} copy(bf16[128,16,128]{2,0,1:T(8,128)(2,1)S(1)} %bitcast.13) | data formatting | bytes 1048576
  69.7 1.0 %copy.15 = f32[16,128,128]{2,1,0:T(8,128)} copy(f32[16,128,128]{2,1,0:T(8,128)S(1)} %get-tuple-element.13) | data formatting | bytes 2097152
  (2 shorter events, 0.0 us)
Async XLA Ops:
  0.6 1.2 %copy-start = (f32[16,128,128]{2,1,0:T(8,128)S(1)}, f32[16,128,128]{2,1,0:T(8,128)}, u32[]{:S(2)}) copy-start(f32[16,128,128]{2,1,0:T(8,128)} %param.7) | copy-start | bytes 3145732
  0.6 1.2 %copy-start.2 = (bf16[128,4,128]{2,1,0:T(4,128)(2,1)S(1)}, bf16[128,4,128]{2,1,0:T(4,128)(2,1)}, u32[]{:S(2)}) copy-start(bf16[128,4,128]{2,1,0:T(4,128)(2,1)} %param.6) | copy-start | bytes 393220
  1.9 1.1 %copy-start.1 = (bf16[128,16,128]{2,1,0:T(8,128)(2,1)S(1)}, bf16[128,16,128]{2,1,0:T(8,128)(2,1)}, u32[]{:S(2)}) copy-start(bf16[128,16,128]{2,1,0:T(8,128)(2,1)} %param.4) | copy-start | bytes 1572868
